TPU v7x, 32 devices: a whole 2x2x4 slice. The times are simulated.
32 devices in a mesh: order: 1, shard: 32 (over z, y, x, core).
Axes of the slice: x: 2, y: 2, z: 4, core: 2. Of those that a mesh axis runs over, the one named last changes fastest.
Arguments:
- sky_coeffs: float32 [32, 2, 2048], P('shard'), may hold values from -6 to 6
- beam_coeffs: float32 [64, 2048], P('order'), may hold values from -0.09375 to 0.09375
- wigner: bfloat16 [32, 64, 2048, 128], P('shard', 'order'), may hold values from -0.125 to 0.125
- visits: int32 [32, 32, 4], P(('order', 'shard')), may hold values from -1 to 511, as said below
- point_slot: int32 [524288], P(('order', 'shard')), may hold values from 0 to 127, as said below
- phi_cell: int32 [524288], P(('order', 'shard')), may hold values from 0 to 30
- psi_cell: int32 [524288], P(('order', 'shard')), may hold values from 0 to 127
- fraction: float32 [2, 524288], P(None, ('order', 'shard')), may hold values from 0 to 1
Outputs:
- timeline: float32 [524288], P(('order', 'shard'))
Inputs may be any that keep to these rules, and one draw needn't show every extreme that they name: Live entries of one row visits[r, d] are distinct tiles of owner d and come first; every row holds 1 to 4 live entries; for every device r some owner d has all 4 entries live. `point_slot`: every pointing names a live entry of its own device's visit list. Of one device's pointings, exactly 768 name each of half of the owners and 256 each of the others.
All inputs are finite; a program needn't handle non-finite values.
Results may differ from a plain program's by a relative error of at most 0.008.
Values may be sent and summed in bfloat16 or wider, within the bound.
A program may use at most 128 MiB of HBM per device.

v0:
```python
import math

import jax
import jax.numpy as jnp
from jax import lax
from jax.sharding import PartitionSpec as P

NPHI = 4096
NPSI = 128
PHI_T = 32


def wave_table(count, modes, first):
    grid = jnp.arange(count, dtype=jnp.int32)[:, None]
    mode = jnp.arange(modes, dtype=jnp.int32)[None, :] + first
    phase = (grid * mode % count).astype(jnp.float32) * (2.0 * math.pi / count)
    return (jnp.cos(phase).astype(jnp.bfloat16), jnp.sin(phase).astype(jnp.bfloat16))


def pick_tiles(table, wanted):
    safe = jnp.maximum(wanted, 0)
    tiles = table[safe]
    return jnp.where(wanted[..., None] >= 0, tiles, jnp.zeros_like(tiles))


def deliver(requests, table):
    return lax.all_to_all(
        pick_tiles(
            table,
            lax.all_to_all(requests, ("order", "shard"), split_axis=0, concat_axis=0, tiled=True),
        ),
        ("order", "shard"),
        split_axis=0,
        concat_axis=0,
        tiled=True,
    )


def blend(corners, fraction):
    along_phi = fraction[0]
    along_psi = fraction[1]
    return (1.0 - along_phi) * (
        (1.0 - along_psi) * corners[0] + along_psi * corners[1]
    ) + along_phi * ((1.0 - along_psi) * corners[2] + along_psi * corners[3])


def shards(sky_coeffs, beam_coeffs, wigner, visits, point_slot, phi_cell, psi_cell, fraction):
    order_count = lax.axis_size("order")
    shard_count = lax.axis_size("shard")
    local_modes = sky_coeffs.shape[0]
    local_orders = beam_coeffs.shape[0]
    theta_count = wigner.shape[3]
    weighted = (sky_coeffs[:, None, :, :] * beam_coeffs[None, :, None, :]).astype(jnp.bfloat16)
    coeffs = jnp.einsum("mkcl,mklt->mtkc", weighted, wigner, preferred_element_type=jnp.float32)
    coeffs = coeffs.astype(jnp.bfloat16).reshape(local_modes, theta_count, local_orders * 2)
    row_count = theta_count // shard_count
    rows = lax.all_to_all(coeffs, "shard", split_axis=1, concat_axis=0, tiled=True)
    mode_count = rows.shape[0]
    rows = rows.reshape(mode_count, row_count, local_orders, 2)
    stacked = jnp.concatenate([rows[..., 0], rows[..., 1]], axis=0).reshape(
        2 * mode_count, row_count * local_orders
    )
    cos_phi, sin_phi = wave_table(NPHI, mode_count, 0)
    phi_table = jnp.concatenate(
        [jnp.concatenate([cos_phi, -sin_phi], axis=1), jnp.concatenate([sin_phi, cos_phi], axis=1)],
        axis=0,
    )
    synth = jnp.dot(phi_table, stacked, preferred_element_type=jnp.float32).astype(jnp.bfloat16)
    synth = synth.reshape(2, NPHI, row_count, local_orders)
    cos_psi, sin_psi = wave_table(NPSI, local_orders, lax.axis_index("order") * local_orders)
    psi_table = jnp.stack([jnp.transpose(cos_psi), -jnp.transpose(sin_psi)], axis=0)
    partial_value = jnp.einsum(
        "cprk,ckq->rpq", synth, psi_table, preferred_element_type=jnp.float32
    )
    partial_bf = partial_value.astype(jnp.bfloat16)
    term = lax.optimization_barrier(partial_bf).astype(jnp.float32)
    cube_part = lax.psum_scatter(
        term.astype(jnp.bfloat16), "order", scatter_dimension=1, tiled=True
    )
    cells = PHI_T * NPSI
    blocks = NPHI // (order_count * PHI_T)
    own_visits = visits[0]
    table = cube_part.reshape(row_count * blocks, cells)
    received = deliver(own_visits, table)
    flat_tiles = received.reshape(-1)
    base = point_slot * cells + phi_cell * NPSI
    next_psi = (psi_cell + 1) % NPSI
    corners = jnp.stack(
        [
            flat_tiles[base + psi_cell],
            flat_tiles[base + next_psi],
            flat_tiles[base + NPSI + psi_cell],
            flat_tiles[base + NPSI + next_psi],
        ],
        axis=0,
    )
    return blend(corners.astype(jnp.float32), fraction)


def solution(mesh):
    placed = (
        P("shard", None, None),
        P("order", None),
        P("shard", "order", None, None),
        P(("order", "shard"), None, None),
        P(("order", "shard")),
        P(("order", "shard")),
        P(("order", "shard")),
        P(None, ("order", "shard")),
    )
    return jax.shard_map(
        shards, mesh=mesh, in_specs=placed, out_specs=P(("order", "shard")), check_vma=False
    )
```

profile of v0, /device:TPU:0, one launch (start us, length us, event | category | flops | bytes accessed | tf_op | source)
XLA Modules:
  0.0 524.7 jit_solution(7316144988281120599)
XLA Ops:
  0.0 1.4 copy.29
  1.4 7.3 %all-to-all-start = ((s32[32,1,4]{2,1,0:T(1,128)}), s32[32,1,4]{2,1,0:T(1,128)S(1)}, u32[]{:S(2)}, u32[]{:S(2)}) async-start(s32[32,1,4]{2,1,0:T(1,128)} %copy.29), calls=%async_computation | async-start | bytes 32768 | tf_op jit(solution)/shard_map/all_to_all | solution.py:30
  8.7 2.2 sine_convert_fusion
  10.9 2.0 fusion.27
  12.8 0.1 cosine_convert_fusion.1
  13.0 13.1 %fusion.9 = bf16[64,2,128]{2,1,0:T(2,128)(2,1)S(1)} fusion(bf16[1,64,2048,128]{3,2,1,0:T(8,128)(2,1)} %param.10, f32[64,2048]{1,0:T(8,128)} %param.9, f32[2,2048]{1,0:T(2,128)} %bitcast.44), kind=kOutput, calls=%fused_computation.12 | convolution fusion | flops 67649536 | bytes 34127872 | tf_op jit(solution)/shard_map/mkcl,mklt->mtkc/dot_general | solution.py:54
  26.1 0.1 fusion.49
  26.2 0.1 copy.32
  26.4 0.5 broadcast.213
  26.9 0.8 reduce.4
  27.7 0.6 reshape.221
  28.3 0.0 all-to-all-done
  28.3 6.0 %all-to-all-start.1 = ((bf16[32,2,256]{2,1,0:T(2,128)(2,1)}), bf16[32,2,256]{2,1,0:T(2,128)(2,1)S(1)}, u32[]{:S(2)}, u32[]{:S(2)}) async-start(bf16[32,2,256]{2,1,0:T(2,128)(2,1)} %reshape.221), calls=%async_computation.1 | async-start | bytes 65536 | tf_op jit(solution)/shard_map/all_to_all | solution.py:57
  34.4 0.1 maximum_reduce_fusion
  34.4 0.1 reshape.167
  34.6 0.1 copy.30
  34.7 0.1 copy.31
  34.8 6.7 %all-to-all-done.1 = bf16[32,2,256]{2,1,0:T(2,128)(2,1)S(1)} async-done(((bf16[32,2,256]{2,1,0:T(2,128)(2,1)}), bf16[32,2,256]{2,1,0:T(2,128)(2,1)S(1)}, u32[]{:S(2)}, u32[]{:S(2)}) %all-to-all-start.1) | async-done | bytes 32800 | tf_op jit(solution)/shard_map/all_to_all | solution.py:57
  41.5 0.1 copy.33
  41.6 2.2 reshape.159
  43.8 0.1 fusion.52
  43.9 0.6 copy.34
  44.6 0.1 concatenate.20
  44.7 0.6 copy.35
  45.3 0.1 concatenate.21
  45.4 3.3 convolution_convert_fusion
  48.7 12.9 %reshape.213 = bf16[2,4096,4,64]{3,2,1,0:T(4,128)(2,1)} reshape(bf16[8192,256]{1,0:T(8,128)(2,1)} %convolution_convert_fusion) | data formatting | bytes 8388608 | tf_op jit(solution)/shard_map/reshape | solution.py:69
  61.6 8.3 %fusion.6 = bf16[4,4096,128]{1,2,0:T(8,128)(2,1)} fusion(bf16[2,4096,4,64]{3,2,1,0:T(4,128)(2,1)} %reshape.213, bf16[1,64,128]{2,1,0:T(8,128)(2,1)S(1)} %fusion.49, bf16[1,64,128]{2,1,0:T(8,128)(2,1)S(1)} %cosine_convert_fusion.1), kind=kOutput, calls=%fused_computation.11 | convolution fusion | flops 539033600 | bytes 8421376 | tf_op jit(solution)/shard_map/cprk,ckq->rpq/dot_general | solution.py:72
  69.9 6.3 %copy.38 = bf16[4,4096,128]{2,1,0:T(8,128)(2,1)} copy(bf16[4,4096,128]{1,2,0:T(8,128)(2,1)} %fusion.6) | data formatting | bytes 8388608 | tf_op jit(solution)/shard_map/optimization_barrier | solution.py:76
  76.2 7.4 %reshape.161 = bf16[512,4096]{1,0:T(8,128)(2,1)} reshape(bf16[4,4096,128]{2,1,0:T(8,128)(2,1)} %copy.38) | data formatting | bytes 8388608 | tf_op jit(solution)/shard_map/reshape | solution.py:83
  83.6 4.9 gather_fusion
  88.5 0.0 copy-start
  88.5 0.0 copy-start.2
  88.6 0.0 copy-start.3
  88.6 0.4 reshape.166
  89.0 1.5 broadcast_select_fusion
  90.5 2.9 all-to-all-start.2
  93.4 0.0 copy-done
  93.4 0.1 fusion.30
  93.5 25.8 %all-to-all-done.2 = bf16[32,4,4096]{2,1,0:T(4,128)(2,1)S(1)} async-done(((bf16[32,4,4096]{2,1,0:T(4,128)(2,1)}), bf16[32,4,4096]{2,1,0:T(4,128)(2,1)S(1)}, u32[]{:S(2)}, u32[]{:S(2)}) %all-to-all-start.2) | async-done | bytes 1048608 | tf_op jit(solution)/shard_map/all_to_all | solution.py:27
  119.3 0.2 copy.42
  119.6 100.9 %gather_fusion.2 = bf16[16384]{0:T(1024)(128)(2,1)S(1)} fusion(bf16[524288]{0:T(1024)(128)(2,1)S(1)} %bitcast.36, s32[16384]{0:T(1024)S(1)} %get-tuple-element.9), kind=kCustom, calls=%fused_computation.2 | custom fusion | bytes 131072 | tf_op jit(solution)/shard_map/gather | solution.py:91
  220.5 100.9 %gather_fusion.3 = bf16[16384]{0:T(1024)(128)(2,1)S(1)} fusion(bf16[524288]{0:T(1024)(128)(2,1)S(1)} %bitcast.37, s32[16384]{0:T(1024)S(1)} %get-tuple-element.10), kind=kCustom, calls=%fused_computation.3 | custom fusion | bytes 131072 | tf_op jit(solution)/shard_map/gather | solution.py:92
  321.5 100.9 %gather_fusion.4 = bf16[16384]{0:T(1024)(128)(2,1)S(1)} fusion(bf16[524288]{0:T(1024)(128)(2,1)S(1)} %bitcast.38, s32[16384]{0:T(1024)S(1)} %get-tuple-element.11), kind=kCustom, calls=%fused_computation.4 | custom fusion | bytes 131072 | tf_op jit(solution)/shard_map/gather | solution.py:93
  422.5 0.0 copy-start.1
  422.5 100.9 %gather_fusion.1 = bf16[16384]{0:T(1024)(128)(2,1)S(1)} fusion(bf16[524288]{0:T(1024)(128)(2,1)S(1)} %bitcast.39, s32[16384]{0:T(1024)S(1)} %get-tuple-element.5), kind=kCustom, calls=%fused_computation.1 | custom fusion | bytes 131072 | tf_op jit(solution)/shard_map/gather | solution.py:90
  523.4 0.3 maximum_convert_fusion
  523.8 1.0 fusion.37
  (11 shorter events, 0.2 us)
Async XLA Ops:
  1.4 27.0 %all-to-all-start = ((s32[32,1,4]{2,1,0:T(1,128)}), s32[32,1,4]{2,1,0:T(1,128)S(1)}, u32[]{:S(2)}, u32[]{:S(2)}) async-start(s32[32,1,4]{2,1,0:T(1,128)} %copy.29), calls=%async_computation | async-start | bytes 32768 | tf_op jit(solution)/shard_map/all_to_all | solution.py:30
  28.3 13.1 %all-to-all-start.1 = ((bf16[32,2,256]{2,1,0:T(2,128)(2,1)}), bf16[32,2,256]{2,1,0:T(2,128)(2,1)S(1)}, u32[]{:S(2)}, u32[]{:S(2)}) async-start(bf16[32,2,256]{2,1,0:T(2,128)(2,1)} %reshape.221), calls=%async_computation.1 | async-start | bytes 65536 | tf_op jit(solution)/shard_map/all_to_all | solution.py:57
  88.5 4.8 copy-start
  88.5 4.8 copy-start.2
  88.6 4.8 copy-start.3
  90.5 28.8 %all-to-all-start.2 = ((bf16[32,4,4096]{2,1,0:T(4,128)(2,1)}), bf16[32,4,4096]{2,1,0:T(4,128)(2,1)S(1)}, u32[]{:S(2)}, u32[]{:S(2)}) async-start(bf16[32,4,4096]{2,1,0:T(4,128)(2,1)} %broadcast_select_fusion), calls=%async_computation.2 | async-start | bytes 2097152 | tf_op jit(solution)/shard_map/all_to_all | solution.py:27
  422.5 101.3 %copy-start.1 = (f32[2,16384]{1,0:T(2,128)S(1)}, f32[2,16384]{1,0:T(2,128)}, u32[]{:S(2)}) copy-start(f32[2,16384]{1,0:T(2,128)} %param.15) | copy-start | bytes 393220
where the time goes:
time: 526 us; the launch traced here: 525 us
  local copies, waits for them, and re-layouts  443 us (84%)
  waiting for transfers between devices  32.5 us (6%)
  matrix products  24.6 us (5%)
  starting transfers between devices  16.2 us (3%)
  other arithmetic  8.21 us (2%)
    gather x1, local copies, waits for them, and re-layouts, shards(): flat_tiles[base + next_psi]  101 us
    gather x1, local copies, waits for them, and re-layouts, shards(): flat_tiles[base + NPSI + psi_cell]  101 us
    gather x1, local copies, waits for them, and re-layouts, shards(): flat_tiles[base + NPSI + next_psi]  101 us
    gather x1, local copies, waits for them, and re-layouts, shards(): flat_tiles[base + psi_cell]  101 us
    all_to_all x1, waiting for transfers between devices, deliver(): lax.all_to_all(pick_tiles(table, lax.all_to_all(requests, ('order', 'shar...  25.8 us
    dot_general x1, matrix products, shards(): jnp.einsum('mkcl,mklt->mtkc', weighted, wigner, preferred_element_type=jn...  13.1 us
    reshape x1, local copies, waits for them, and re-layouts, shards(): synth = synth.reshape(2, NPHI, row_count, local_orders)  12.9 us
  transfers between devices with their start and end apart: 3, of which 2 were waited for; matrix products, arithmetic and copies ran while one was open for 4% of the time, Pallas kernels for 0%

commit v1 on v0

v1 whole, which is shorter than its diff:
```python
import functools
import math

import jax
import jax.numpy as jnp
from jax import lax
from jax.experimental import pallas as pl
from jax.experimental.pallas import tpu as pltpu
from jax.sharding import PartitionSpec as P

NPHI = 4096
NPSI = 128
PHI_T = 32
LOW = 8
LANES = 128
CHUNK = 256


def wave_table(count, grid, mode):
    phase = ((grid * mode) % count).astype(jnp.float32) * (2.0 * math.pi / count)
    return jnp.cos(phase), jnp.sin(phase)


def interpolate(
    modes,
    orders,
    coeffs_ref,
    row_ref,
    turn_cos_ref,
    turn_sin_ref,
    phi_table_ref,
    psi_table_ref,
    slot_ref,
    phi_ref,
    psi_ref,
    fraction_ref,
    out_ref,
    picked,
    edge,
    synth,
    wave,
):
    terms = 2 * orders
    high = PHI_T // LOW
    theta, slots = coeffs_ref.shape[1], row_ref.shape[1]
    groups = slots // LANES
    for g in range(groups):
        lanes = slice(g * LANES, (g + 1) * LANES)
        chosen = (
            lax.broadcasted_iota(jnp.int32, (theta, LANES), 0) == row_ref[:, lanes]
        ).astype(jnp.float32).astype(jnp.bfloat16)

        def pick(m, carry):
            rows = pl.ds(pl.multiple_of(m * 4 * terms, 4 * terms), 4 * terms)
            picked[rows, :] = jnp.dot(
                coeffs_ref[rows, :], chosen, preferred_element_type=jnp.float32
            )
            return carry

        lax.fori_loop(0, modes // 4, pick, 0)
        turn_cos, turn_sin = turn_cos_ref[:, lanes], turn_sin_ref[:, lanes]

        def sum_modes(k, carry):
            real = picked[pl.ds(2 * k, modes, stride=terms), :]
            imag = picked[pl.ds(2 * k + 1, modes, stride=terms), :]
            turned = jnp.concatenate(
                [turn_cos * real - turn_sin * imag, turn_sin * real + turn_cos * imag], axis=0
            ).astype(jnp.bfloat16)
            values = jnp.dot(phi_table_ref[...], turned, preferred_element_type=jnp.float32)
            for h in range(high):
                synth[
                    pl.ds(pl.multiple_of(k * 2 * LOW, 2 * LOW), 2 * LOW),
                    h * slots + g * LANES : h * slots + (g + 1) * LANES,
                ] = values[h * 2 * LOW : (h + 1) * 2 * LOW].astype(jnp.bfloat16)
            edge[pl.ds(pl.multiple_of(k * 2 * high, 2 * high), 2 * high), :] = values[
                2 * PHI_T :
            ]
            return carry

        lax.fori_loop(0, orders, sum_modes, 0, unroll=4)
        for part in range(2):
            for h in range(high):
                synth[
                    terms * LOW + part * orders : terms * LOW + (part + 1) * orders,
                    h * slots + g * LANES : h * slots + (g + 1) * LANES,
                ] = edge[pl.ds(part * high + h, orders, stride=2 * high), :].astype(jnp.bfloat16)

    def chunk(i, carry):
        phi, psi = phi_ref[i], psi_ref[i]
        along = fraction_ref[i]
        along_phi, along_psi = along[0:1], along[1:2]
        key = (phi // LOW) * slots + slot_ref[i]
        entry = (
            lax.broadcasted_iota(jnp.int32, (high * slots, CHUNK), 0) == key
        ).astype(jnp.float32).astype(jnp.bfloat16)
        at_psi = lax.broadcasted_iota(jnp.int32, (NPSI, CHUNK), 0)
        weight = jnp.where(
            at_psi == psi, 1.0 - along_psi, jnp.where(at_psi == (psi + 1) % NPSI, along_psi, 0.0)
        )
        coarse = weight.astype(jnp.bfloat16)
        fine = (weight - coarse.astype(jnp.float32)).astype(jnp.bfloat16)
        waves = jnp.dot(
            psi_table_ref[...],
            jnp.concatenate([coarse, fine], axis=0),
            preferred_element_type=jnp.float32,
        )
        wave[...] = waves
        values = jnp.dot(synth[...], entry, preferred_element_type=jnp.float32)
        sums = [jnp.zeros((LOW, CHUNK), jnp.float32) for _ in range(4)]
        for k in range(orders):
            for part in range(2):
                at = (2 * k + part) * LOW
                line = part * orders + k
                sums[at // LOW % 4] += values[at : at + LOW] * wave[line : line + 1, :]
        inner = (sums[0] + sums[1]) + (sums[2] + sums[3])
        last = jnp.sum(values[terms * LOW :] * waves, axis=0, keepdims=True)
        low = phi % LOW
        at_low = lax.broadcasted_iota(jnp.int32, (LOW, CHUNK), 0)
        weight_phi = jnp.where(
            at_low == low, 1.0 - along_phi, jnp.where(at_low == low + 1, along_phi, 0.0)
        )
        total = jnp.sum(inner * weight_phi, axis=0, keepdims=True)
        out_ref[i] = total + jnp.where(low == LOW - 1, along_phi, 0.0) * last
        return carry

    lax.fori_loop(0, slot_ref.shape[0], chunk, 0)


def phi_rows(modes):
    mode = jnp.arange(modes, dtype=jnp.int32)[None, :]
    high = PHI_T // LOW
    cos, sin = wave_table(NPHI, jnp.arange(PHI_T, dtype=jnp.int32)[:, None], mode)
    real = jnp.concatenate([cos, -sin], axis=1)
    imag = jnp.concatenate([sin, cos], axis=1)
    inner = jnp.stack(
        [real.reshape(high, LOW, 2 * modes), imag.reshape(high, LOW, 2 * modes)], axis=1
    ).reshape(2 * PHI_T, 2 * modes)
    zero = jnp.zeros((1, 2 * modes), jnp.float32)
    edge = jnp.concatenate([real[LOW::LOW], zero, imag[LOW::LOW], zero], axis=0)
    return jnp.concatenate([inner, edge], axis=0).astype(jnp.bfloat16)


def psi_rows(orders):
    order = jnp.arange(orders, dtype=jnp.int32)[:, None]
    cos, sin = wave_table(NPSI, jnp.arange(NPSI, dtype=jnp.int32)[None, :], order)
    half = jnp.concatenate([cos, -sin], axis=0).astype(jnp.bfloat16)
    return jnp.concatenate([half, half], axis=1)


def shards(sky_coeffs, beam_coeffs, wigner, visits, point_slot, phi_cell, psi_cell, fraction):
    order_count = lax.axis_size("order")
    shard_count = lax.axis_size("shard")
    local_modes = sky_coeffs.shape[0]
    local_orders = beam_coeffs.shape[0]
    theta_count = wigner.shape[3]
    orders = local_orders * order_count
    modes = local_modes * shard_count
    weighted = (sky_coeffs[:, None, :, :] * beam_coeffs[None, :, None, :]).astype(jnp.bfloat16)
    coeffs = jnp.einsum("mkcl,mklt->mkct", weighted, wigner, preferred_element_type=jnp.float32)
    coeffs = coeffs.astype(jnp.bfloat16).reshape(local_modes * local_orders * 2, theta_count)
    coeffs = lax.all_gather(coeffs, "shard", axis=0, tiled=True)
    if order_count > 1:
        coeffs = coeffs.reshape(modes, local_orders * 2, theta_count)
        coeffs = lax.all_gather(coeffs, "order", axis=1, tiled=True)
        coeffs = coeffs.reshape(modes * orders * 2, theta_count)

    blocks = NPHI // (order_count * PHI_T)
    owners, depth = visits.shape[1], visits.shape[2]
    slots = owners * depth
    tile = jnp.maximum(visits[0], 0).reshape(1, slots)
    owner = (jnp.arange(slots, dtype=jnp.int32) // depth)[None, :]
    row = (owner % shard_count) * (theta_count // shard_count) + tile // blocks
    first_phi = (owner // shard_count) * (NPHI // order_count) + (tile % blocks) * PHI_T
    turn_cos, turn_sin = wave_table(
        NPHI, first_phi, jnp.arange(modes, dtype=jnp.int32)[:, None]
    )
    count = point_slot.shape[0]
    chunks = count // CHUNK
    lined = (chunks, 1, CHUNK)
    pairs = jnp.transpose(fraction.reshape(2, chunks, CHUNK), (1, 0, 2))
    high = PHI_T // LOW
    timeline = pl.pallas_call(
        functools.partial(interpolate, modes, orders),
        out_shape=jax.ShapeDtypeStruct(lined, jnp.float32),
        in_specs=[pl.BlockSpec(memory_space=pltpu.VMEM)] * 10,
        out_specs=pl.BlockSpec(memory_space=pltpu.VMEM),
        scratch_shapes=[
            pltpu.VMEM((modes * orders * 2, LANES), jnp.float32),
            pltpu.VMEM((orders * 2 * high, LANES), jnp.float32),
            pltpu.VMEM((orders * 2 * (LOW + 1), high * slots), jnp.bfloat16),
            pltpu.VMEM((orders * 2, CHUNK), jnp.float32),
        ],
    )(
        coeffs,
        row,
        turn_cos,
        turn_sin,
        phi_rows(modes),
        psi_rows(orders),
        point_slot.reshape(lined),
        phi_cell.reshape(lined),
        psi_cell.reshape(lined),
        pairs,
    )
    return timeline.reshape(count)


def solution(mesh):
    placed = (
        P("shard", None, None),
        P("order", None),
        P("shard", "order", None, None),
        P(("order", "shard"), None, None),
        P(("order", "shard")),
        P(("order", "shard")),
        P(("order", "shard")),
        P(None, ("order", "shard")),
    )
    return jax.shard_map(
        shards, mesh=mesh, in_specs=placed, out_specs=P(("order", "shard")), check_vma=False
    )
```

time: 526 us -> 125 us (0.24)
  local copies, waits for them, and re-layouts: 443 us -> 1.9 us
  Pallas kernels: 0 us -> 41.5 us
  waiting for transfers between devices: 32.5 us -> 52 us
  starting transfers between devices: 16.2 us -> 0.01 us
  between operations: 0.29 us -> 13.4 us
  matrix products: 24.6 us -> 13.7 us
  other arithmetic: 8.21 us -> 2.59 us
    gather x6 -> x0, local copies, waits for them, and re-layouts: 409 us -> none  [the longest x1 101 us: shards(): flat_tiles[base + next_psi]]
    all_gather x0 -> x1, waiting for transfers between devices: none -> 51.9 us  [shards(): coeffs = lax.all_gather(coeffs, 'shard', axis=0, tiled=True)]
    pallas_call x0 -> x1, Pallas kernels: none -> 41.5 us  [shards(): pl.pallas_call(functools.partial(interpolate, modes, orders), out_shape=j...]
    all_to_all x3 -> x0, waiting for transfers between devices: 32.5 us -> none  [the longest x1 25.8 us: deliver(): lax.all_to_all(pick_tiles(table, lax.all_to_all(requests, ('order', 'shar...]
    reshape x4 -> x0, local copies, waits for them, and re-layouts: 22.7 us -> none  [the longest x1 12.9 us: shards(): synth = synth.reshape(2, NPHI, row_count, local_orders)]
    all_to_all x3 -> x0, starting transfers between devices: 16.2 us -> none  [the longest x1 7.33 us: deliver(): lax.all_to_all(requests, ('order', 'shard'), split_axis=0, concat_axis=0,...]
    dot_general x3 -> x1, matrix products: 24.6 us -> 13.7 us  [shards(): jnp.einsum('mkcl,mklt->mkct', weighted, wigner, preferred_element_type=jn...]
    optimization_barrier x1 -> x0, local copies, waits for them, and re-layouts: 6.32 us -> none  [shards(): term = lax.optimization_barrier(partial_bf).astype(jnp.float32)]
  transfers between devices with their start and end apart: 3 -> 1, of which waited for: 2 -> 1; matrix products, arithmetic and copies ran while one was open for 4% -> 4% of each run, Pallas kernels for 0% -> 0%
where the time goes in v1:
time: 125 us
  waiting for transfers between devices  52 us (42%)
  Pallas kernels  41.5 us (33%)
  matrix products  13.7 us (11%)
  between operations  13.4 us (11%)
  other arithmetic  2.59 us (2%)
  local copies, waits for them, and re-layouts  1.9 us (2%)
    all_gather x1, waiting for transfers between devices, shards(): coeffs = lax.all_gather(coeffs, 'shard', axis=0, tiled=True)  51.9 us
    pallas_call x1, Pallas kernels, shards(): pl.pallas_call(functools.partial(interpolate, modes, orders), out_shape=j...  41.5 us
    dot_general x1, matrix products, shards(): jnp.einsum('mkcl,mklt->mkct', weighted, wigner, preferred_element_type=jn...  13.7 us
  transfers between devices with their start and end apart: 1, of which 1 were waited for; matrix products, arithmetic and copies ran while one was open for 4% of the time, Pallas kernels for 0%

profile of v1, /device:TPU:0, one launch (start us, length us, event | category | flops | bytes accessed | tf_op | source)
XLA Modules:
  0.0 125.1 jit_solution(1481090225656442701)
XLA Ops:
  6.5 0.0 copy-start
  6.5 0.0 all-gather.2.cloned.1.call-start
  6.5 13.7 %fusion.2 = bf16[64,2,128]{2,1,0:T(2,128)(2,1)} fusion(bf16[1,64,2048,128]{3,2,1,0:T(8,128)(2,1)} %param.10, f32[64,2048]{1,0:T(8,128)} %param.9, f32[2,2048]{1,0:T(2,128)} %bitcast.21), kind=kOutput, calls=%fused_computation.2 | convolution fusion | flops 67649536 | bytes 34127872 | tf_op jit(solution)/shard_map/mkcl,mklt->mkct/dot_general | solution.py:159
  20.2 0.0 all-gather.2.cloned.1.call-update
  20.2 0.0 copy-done
  20.3 0.1 copy.12
  20.4 0.1 and.161
  20.5 0.1 copy.14
  20.6 0.1 rem.253
  20.7 0.1 copy.13
  20.8 0.1 div.36
  20.9 0.1 fusion.32
  21.0 0.1 negate_convert_fusion.1
  21.1 0.1 pad_maximum_fusion.1
  21.2 0.2 negate_convert_fusion.2
  21.4 0.1 maximum_maximum_fusion.1
  21.5 1.2 concatenate.31.phi_table_ref
  22.7 0.2 negate_convert_fusion
  22.9 0.6 maximum_maximum_fusion.psi_table_ref
  23.5 0.6 fusion.38.row_ref
  24.1 0.7 fusion.35
  24.8 51.9 %all-gather.2.cloned.1.call-done.coeffs_ref = bf16[4096,128]{1,0:T(8,128)(2,1)} async-done(((bf16[128,128]{1,0:T(8,128)(2,1)}), bf16[4096,128]{1,0:T(8,128)(2,1)}) %all-gather.2.cloned.1.call-update) | async-done | bytes 1048592 | tf_op jit(solution)/shard_map/all_gather | solution.py:161
  76.7 41.5 %shard_map.82 = f32[64,1,256]{2,1,0:T(1,128)} custom-call(bf16[4096,128]{1,0:T(8,128)(2,1)} %all-gather.2.cloned.1.call-done.coeffs_ref, s32[1,128]{1,0:T(1,128)} %fusion.38.row_ref, f32[32,128]{1,0:T(8,128)} %get-tuple-element.13.turn_cos_ref, f32[32,128]{1,0:T(8,128)} %get-tuple-element.12.turn_sin_ref, bf16[72,64]{1,0:T(8,128)(2,1)} %concatenate.31.phi_table_ref, ...), custom_call_target="tpu_custom_call" | custom-call | tf_op jit(solution)/shard_map/pallas_call | solution.py:182
  (7 shorter events, 0.1 us)
Async XLA Ops:
  6.5 13.7 %copy-start = (s32[1,32,4]{1,2,0:T(4,128)S(1)}, s32[1,32,4]{1,2,0:T(4,128)}, u32[]{:S(2)}) copy-start(s32[1,32,4]{1,2,0:T(4,128)} %param.11) | copy-start | bytes 1540
  6.5 70.2 %all-gather.2.cloned.1.call-start = ((), (), s32[]{:S(2)}) async-start(), calls=%async_computation | async-start | bytes 1081344 | tf_op jit(solution)/shard_map/all_gather | solution.py:161
Sparse Core Ops, SparseCore 0:
  20.4 56.3 all-gather.1

commit v2 on v1

--- a/solution.py
+++ b/solution.py
@@ -3,6 +3,7 @@
 
 import jax
 import jax.numpy as jnp
+import numpy as np
 from jax import lax
 from jax.experimental import pallas as pl
 from jax.experimental.pallas import tpu as pltpu
@@ -16,18 +17,93 @@
 CHUNK = 256
 
 
+SQUARE = 4
+CORES = 2
+
+
+def gather_blocks(lines, block_ref, out_ref, send_sem, recv_sem):
+    me = lax.axis_index("shard")
+    core = me % CORES
+    square = me // CORES % SQUARE
+    line = me // (CORES * SQUARE)
+    depth = block_ref.shape[0]
+
+    def index(at_line, at_square, at_core):
+        return (at_line * SQUARE + at_square) * CORES + at_core
+
+    along = [(line + d) % lines for d in range(1, lines)]
+    across = [(square + d) % SQUARE for d in range(1, SQUARE)]
+    other = (core + 1) % CORES
+    line_peers = [index(a, square, core) for a in along]
+    square_peers = [index(line, b, core) for b in across]
+    twin = index(line, square, other)
+    barrier = pltpu.get_barrier_semaphore()
+    peers = line_peers + square_peers + [twin]
+    for peer in peers:
+        pl.semaphore_signal(
+            barrier, inc=1, device_id={"shard": peer}, device_id_type=pl.DeviceIdType.MESH
+        )
+    pl.semaphore_wait(barrier, len(peers))
+
+    started = []
+
+    def place(owner):
+        return out_ref.at[pl.ds(pl.multiple_of(owner * depth, depth), depth), :]
+
+    def send(source, owner, peer):
+        copy = pltpu.make_async_remote_copy(
+            src_ref=source,
+            dst_ref=place(owner),
+            send_sem=send_sem.at[len(started)],
+            recv_sem=recv_sem.at[owner],
+            device_id={"shard": peer},
+            device_id_type=pl.DeviceIdType.MESH,
+        )
+        copy.start()
+        started.append(copy)
+
+    def arrive(owner):
+        pltpu.make_async_remote_copy(
+            src_ref=place(owner),
+            dst_ref=place(owner),
+            send_sem=send_sem.at[0],
+            recv_sem=recv_sem.at[owner],
+            device_id={"shard": twin},
+            device_id_type=pl.DeviceIdType.MESH,
+        ).wait_recv()
+
+    for peer in line_peers + square_peers + [twin]:
+        send(block_ref, me, peer)
+    out_ref[pl.ds(pl.multiple_of(me * depth, depth), depth), :] = block_ref[...]
+    for owner in line_peers:
+        arrive(owner)
+        for peer in square_peers + [twin]:
+            send(place(owner), owner, peer)
+    for a in [line] + along:
+        for b in across:
+            owner = index(a, b, core)
+            arrive(owner)
+            send(place(owner), owner, twin)
+    for a in [line] + along:
+        for b in [square] + across:
+            arrive(index(a, b, other))
+    for copy in started:
+        copy.wait_send()
+
+
 def wave_table(count, grid, mode):
-    phase = ((grid * mode) % count).astype(jnp.float32) * (2.0 * math.pi / count)
-    return jnp.cos(phase), jnp.sin(phase)
+    phase = 2.0 * math.pi * ((grid * mode) % count) / count
+    return np.cos(phase), np.sin(phase)
 
 
 def interpolate(
     modes,
     orders,
+    order_count,
+    shard_count,
+    depth,
     coeffs_ref,
-    row_ref,
-    turn_cos_ref,
-    turn_sin_ref,
+    visit_ref,
     phi_table_ref,
     psi_table_ref,
     slot_ref,
@@ -42,12 +118,17 @@
 ):
     terms = 2 * orders
     high = PHI_T // LOW
-    theta, slots = coeffs_ref.shape[1], row_ref.shape[1]
+    theta, slots = coeffs_ref.shape[1], visit_ref.shape[1]
+    blocks = NPHI // (order_count * PHI_T)
     groups = slots // LANES
     for g in range(groups):
         lanes = slice(g * LANES, (g + 1) * LANES)
+        tile = jnp.maximum(visit_ref[:, lanes], 0)
+        owner = (lax.broadcasted_iota(jnp.int32, (1, LANES), 1) + g * LANES) // depth
+        row = (owner % shard_count) * (theta // shard_count) + tile // blocks
+        first_phi = (owner // shard_count) * (NPHI // order_count) + (tile % blocks) * PHI_T
         chosen = (
-            lax.broadcasted_iota(jnp.int32, (theta, LANES), 0) == row_ref[:, lanes]
+            lax.broadcasted_iota(jnp.int32, (theta, LANES), 0) == row
         ).astype(jnp.float32).astype(jnp.bfloat16)
 
         def pick(m, carry):
@@ -58,7 +139,9 @@
             return carry
 
         lax.fori_loop(0, modes // 4, pick, 0)
-        turn_cos, turn_sin = turn_cos_ref[:, lanes], turn_sin_ref[:, lanes]
+        turn = (lax.broadcasted_iota(jnp.int32, (modes, LANES), 0) * first_phi) % NPHI
+        angle = turn.astype(jnp.float32) * (2.0 * math.pi / NPHI)
+        turn_cos, turn_sin = jnp.cos(angle), jnp.sin(angle)
 
         def sum_modes(k, carry):
             real = picked[pl.ds(2 * k, modes, stride=terms), :]
@@ -127,24 +210,24 @@
 
 
 def phi_rows(modes):
-    mode = jnp.arange(modes, dtype=jnp.int32)[None, :]
+    mode = np.arange(modes, dtype=np.int64)[None, :]
     high = PHI_T // LOW
-    cos, sin = wave_table(NPHI, jnp.arange(PHI_T, dtype=jnp.int32)[:, None], mode)
-    real = jnp.concatenate([cos, -sin], axis=1)
-    imag = jnp.concatenate([sin, cos], axis=1)
-    inner = jnp.stack(
+    cos, sin = wave_table(NPHI, np.arange(PHI_T, dtype=np.int64)[:, None], mode)
+    real = np.concatenate([cos, -sin], axis=1)
+    imag = np.concatenate([sin, cos], axis=1)
+    inner = np.stack(
         [real.reshape(high, LOW, 2 * modes), imag.reshape(high, LOW, 2 * modes)], axis=1
     ).reshape(2 * PHI_T, 2 * modes)
-    zero = jnp.zeros((1, 2 * modes), jnp.float32)
-    edge = jnp.concatenate([real[LOW::LOW], zero, imag[LOW::LOW], zero], axis=0)
-    return jnp.concatenate([inner, edge], axis=0).astype(jnp.bfloat16)
+    zero = np.zeros((1, 2 * modes), np.float64)
+    edge = np.concatenate([real[LOW::LOW], zero, imag[LOW::LOW], zero], axis=0)
+    return jnp.asarray(np.concatenate([inner, edge], axis=0), jnp.bfloat16)
 
 
 def psi_rows(orders):
-    order = jnp.arange(orders, dtype=jnp.int32)[:, None]
-    cos, sin = wave_table(NPSI, jnp.arange(NPSI, dtype=jnp.int32)[None, :], order)
-    half = jnp.concatenate([cos, -sin], axis=0).astype(jnp.bfloat16)
-    return jnp.concatenate([half, half], axis=1)
+    order = np.arange(orders, dtype=np.int64)[:, None]
+    cos, sin = wave_table(NPSI, np.arange(NPSI, dtype=np.int64)[None, :], order)
+    half = np.concatenate([cos, -sin], axis=0)
+    return jnp.asarray(np.concatenate([half, half], axis=1), jnp.bfloat16)
 
 
 def shards(sky_coeffs, beam_coeffs, wigner, visits, point_slot, phi_cell, psi_cell, fraction):
@@ -158,31 +241,34 @@
     weighted = (sky_coeffs[:, None, :, :] * beam_coeffs[None, :, None, :]).astype(jnp.bfloat16)
     coeffs = jnp.einsum("mkcl,mklt->mkct", weighted, wigner, preferred_element_type=jnp.float32)
     coeffs = coeffs.astype(jnp.bfloat16).reshape(local_modes * local_orders * 2, theta_count)
-    coeffs = lax.all_gather(coeffs, "shard", axis=0, tiled=True)
+    coeffs = pl.pallas_call(
+        functools.partial(gather_blocks, shard_count // (SQUARE * CORES)),
+        out_shape=jax.ShapeDtypeStruct((shard_count * coeffs.shape[0], theta_count), jnp.bfloat16),
+        in_specs=[pl.BlockSpec(memory_space=pltpu.VMEM)],
+        out_specs=pl.BlockSpec(memory_space=pltpu.VMEM),
+        scratch_shapes=[
+            pltpu.SemaphoreType.DMA((shard_count - 1,)),
+            pltpu.SemaphoreType.DMA((shard_count,)),
+        ],
+        compiler_params=pltpu.CompilerParams(collective_id=0, has_side_effects=True),
+    )(coeffs)
     if order_count > 1:
         coeffs = coeffs.reshape(modes, local_orders * 2, theta_count)
         coeffs = lax.all_gather(coeffs, "order", axis=1, tiled=True)
         coeffs = coeffs.reshape(modes * orders * 2, theta_count)
 
-    blocks = NPHI // (order_count * PHI_T)
-    owners, depth = visits.shape[1], visits.shape[2]
-    slots = owners * depth
-    tile = jnp.maximum(visits[0], 0).reshape(1, slots)
-    owner = (jnp.arange(slots, dtype=jnp.int32) // depth)[None, :]
-    row = (owner % shard_count) * (theta_count // shard_count) + tile // blocks
-    first_phi = (owner // shard_count) * (NPHI // order_count) + (tile % blocks) * PHI_T
-    turn_cos, turn_sin = wave_table(
-        NPHI, first_phi, jnp.arange(modes, dtype=jnp.int32)[:, None]
-    )
+    slots = visits.shape[1] * visits.shape[2]
     count = point_slot.shape[0]
     chunks = count // CHUNK
     lined = (chunks, 1, CHUNK)
     pairs = jnp.transpose(fraction.reshape(2, chunks, CHUNK), (1, 0, 2))
     high = PHI_T // LOW
     timeline = pl.pallas_call(
-        functools.partial(interpolate, modes, orders),
+        functools.partial(
+            interpolate, modes, orders, order_count, shard_count, visits.shape[2]
+        ),
         out_shape=jax.ShapeDtypeStruct(lined, jnp.float32),
-        in_specs=[pl.BlockSpec(memory_space=pltpu.VMEM)] * 10,
+        in_specs=[pl.BlockSpec(memory_space=pltpu.VMEM)] * 8,
         out_specs=pl.BlockSpec(memory_space=pltpu.VMEM),
         scratch_shapes=[
             pltpu.VMEM((modes * orders * 2, LANES), jnp.float32),
@@ -192,9 +278,7 @@
         ],
     )(
         coeffs,
-        row,
-        turn_cos,
-        turn_sin,
+        visits.reshape(1, slots),
         phi_rows(modes),
         psi_rows(orders),
         point_slot.reshape(lined),

time: 125 us -> 74.5 us (0.60)
  waiting for transfers between devices: 52 us -> 0 us
  Pallas kernels: 41.5 us -> 59.2 us
  between operations: 13.4 us -> 0.01 us
  other arithmetic: 2.59 us -> 0 us
    all_gather x1 -> x0, waiting for transfers between devices: 51.9 us -> none  [shards(): coeffs = lax.all_gather(coeffs, 'shard', axis=0, tiled=True)]
    pallas_call x1 -> x2, Pallas kernels: 41.5 us -> 59.2 us  [the longest x1 41.6 us: shards(): pl.pallas_call(functools.partial(interpolate, modes, orders, order_count,...]
  transfers between devices with their start and end apart: 1 -> 0, of which waited for: 1 -> 0; matrix products, arithmetic and copies ran while one was open for 4% -> 0% of each run, Pallas kernels for 0% -> 0%
where the time goes in v2:
time: 74.5 us; the launch traced here: 74.3 us
  Pallas kernels  59.2 us (79%)
  matrix products  13.7 us (18%)
  local copies, waits for them, and re-layouts  1.46 us (2%)
    pallas_call x1, Pallas kernels, shards(): pl.pallas_call(functools.partial(interpolate, modes, orders, order_count,...  41.6 us
    pallas_call x1, Pallas kernels, shards(): pl.pallas_call(functools.partial(gather_blocks, shard_count // (SQUARE *...  17.5 us
    dot_general x1, matrix products, shards(): jnp.einsum('mkcl,mklt->mkct', weighted, wigner, preferred_element_type=jn...  13.7 us

profile of v2, /device:TPU:0, one launch (start us, length us, event | category | flops | bytes accessed | tf_op | source)
XLA Modules:
  0.0 74.3 jit_solution(9586105911302905355)
XLA Ops:
  0.0 0.8 %copy.12 = s32[1,32,4]{2,1,0:T(8,128)S(1)} copy(s32[1,32,4]{1,2,0:T(4,128)} %param.13) | data formatting | bytes 1024 | tf_op args[3]
  0.8 0.7 reshape.38.visit_ref
  1.5 13.7 %fusion.2 = bf16[64,2,128]{2,1,0:T(2,128)(2,1)} fusion(bf16[1,64,2048,128]{3,2,1,0:T(8,128)(2,1)} %param.12, f32[64,2048]{1,0:T(8,128)} %param.11, f32[2,2048]{1,0:T(2,128)} %bitcast.19), kind=kOutput, calls=%fused_computation.2 | convolution fusion | flops 67649536 | bytes 34127872 | tf_op jit(solution)/shard_map/mkcl,mklt->mkct/dot_general | solution.py:242
  15.1 17.5 %shard_map.100.coeffs_ref = bf16[4096,128]{1,0:T(8,128)(2,1)} custom-call(bf16[128,128]{1,0:T(8,128)(2,1)} %bitcast.14), custom_call_target="tpu_custom_call" | custom-call | tf_op jit(solution)/shard_map/pallas_call | solution.py:244
  32.7 41.6 %shard_map.101 = f32[64,1,256]{2,1,0:T(1,128)} custom-call(bf16[4096,128]{1,0:T(8,128)(2,1)} %shard_map.100.coeffs_ref, s32[1,128]{1,0:T(1,128)} %reshape.38.visit_ref, bf16[72,64]{1,0:T(8,128)(2,1)} %constant.4.clone.phi_table_ref, bf16[128,256]{1,0:T(8,128)(2,1)} %constant.5.clone.psi_table_ref, s32[64,1,256]{2,1,0:T(1,128)} %bitcast.16, ...), custom_call_target="tpu_custom_call" | custom-call | tf_op jit(solution)/shard_map/pallas_call | solution.py:266

commit v3 on v2

--- a/solution.py
+++ b/solution.py
@@ -114,7 +114,10 @@
     picked,
     edge,
     synth,
-    wave,
+    wave_a,
+    wave_b,
+    values_a,
+    values_b,
 ):
     terms = 2 * orders
     high = PHI_T // LOW
@@ -168,10 +171,9 @@
                     h * slots + g * LANES : h * slots + (g + 1) * LANES,
                 ] = edge[pl.ds(part * high + h, orders, stride=2 * high), :].astype(jnp.bfloat16)
 
-    def chunk(i, carry):
+    def begin(i, values, wave):
         phi, psi = phi_ref[i], psi_ref[i]
-        along = fraction_ref[i]
-        along_phi, along_psi = along[0:1], along[1:2]
+        along_psi = fraction_ref[i][1:2]
         key = (phi // LOW) * slots + slot_ref[i]
         entry = (
             lax.broadcasted_iota(jnp.int32, (high * slots, CHUNK), 0) == key
@@ -182,21 +184,24 @@
         )
         coarse = weight.astype(jnp.bfloat16)
         fine = (weight - coarse.astype(jnp.float32)).astype(jnp.bfloat16)
-        waves = jnp.dot(
+        wave[...] = jnp.dot(
             psi_table_ref[...],
             jnp.concatenate([coarse, fine], axis=0),
             preferred_element_type=jnp.float32,
         )
-        wave[...] = waves
-        values = jnp.dot(synth[...], entry, preferred_element_type=jnp.float32)
+        values[...] = jnp.dot(synth[...], entry, preferred_element_type=jnp.float32)
+
+    def finish(i, values, wave):
+        phi = phi_ref[i]
+        along_phi = fraction_ref[i][0:1]
         sums = [jnp.zeros((LOW, CHUNK), jnp.float32) for _ in range(4)]
         for k in range(orders):
             for part in range(2):
                 at = (2 * k + part) * LOW
                 line = part * orders + k
-                sums[at // LOW % 4] += values[at : at + LOW] * wave[line : line + 1, :]
+                sums[at // LOW % 4] += values[at : at + LOW, :] * wave[line : line + 1, :]
         inner = (sums[0] + sums[1]) + (sums[2] + sums[3])
-        last = jnp.sum(values[terms * LOW :] * waves, axis=0, keepdims=True)
+        last = jnp.sum(values[terms * LOW :, :] * wave[...], axis=0, keepdims=True)
         low = phi % LOW
         at_low = lax.broadcasted_iota(jnp.int32, (LOW, CHUNK), 0)
         weight_phi = jnp.where(
@@ -204,9 +209,18 @@
         )
         total = jnp.sum(inner * weight_phi, axis=0, keepdims=True)
         out_ref[i] = total + jnp.where(low == LOW - 1, along_phi, 0.0) * last
+
+    chunks = slot_ref.shape[0]
+    begin(0, values_a, wave_a)
+
+    def pair(i, carry):
+        begin(2 * i + 1, values_b, wave_b)
+        finish(2 * i, values_a, wave_a)
+        begin(jnp.minimum(2 * i + 2, chunks - 1), values_a, wave_a)
+        finish(2 * i + 1, values_b, wave_b)
         return carry
 
-    lax.fori_loop(0, slot_ref.shape[0], chunk, 0)
+    lax.fori_loop(0, chunks // 2, pair, 0)
 
 
 def phi_rows(modes):
@@ -275,6 +289,9 @@
             pltpu.VMEM((orders * 2 * high, LANES), jnp.float32),
             pltpu.VMEM((orders * 2 * (LOW + 1), high * slots), jnp.bfloat16),
             pltpu.VMEM((orders * 2, CHUNK), jnp.float32),
+            pltpu.VMEM((orders * 2, CHUNK), jnp.float32),
+            pltpu.VMEM((orders * 2 * (LOW + 1), CHUNK), jnp.float32),
+            pltpu.VMEM((orders * 2 * (LOW + 1), CHUNK), jnp.float32),
         ],
     )(
         coeffs,

time: 74.5 us -> 69.9 us (0.938)
  Pallas kernels: 59.2 us -> 54.5 us
    pallas_call x1, Pallas kernels: 41.6 us -> 37 us  [shards(): pl.pallas_call(functools.partial(interpolate, modes, orders, order_count,...]
where the time goes in v3:
time: 69.9 us; the launch traced here: 69.6 us
  Pallas kernels  54.5 us (78%)
  matrix products  13.7 us (20%)
  local copies, waits for them, and re-layouts  1.46 us (2%)
    pallas_call x1, Pallas kernels, shards(): pl.pallas_call(functools.partial(interpolate, modes, orders, order_count,...  37 us
    pallas_call x1, Pallas kernels, shards(): pl.pallas_call(functools.partial(gather_blocks, shard_count // (SQUARE *...  17.5 us
    dot_general x1, matrix products, shards(): jnp.einsum('mkcl,mklt->mkct', weighted, wigner, preferred_element_type=jn...  13.7 us

profile of v3, /device:TPU:0, one launch (start us, length us, event | category | flops | bytes accessed | tf_op | source)
XLA Modules:
  0.0 69.6 jit_solution(10603149257732917709)
XLA Ops:
  0.0 0.8 %copy.12 = s32[1,32,4]{2,1,0:T(8,128)S(1)} copy(s32[1,32,4]{1,2,0:T(4,128)} %param.13) | data formatting | bytes 1024 | tf_op args[3]
  0.8 0.7 reshape.38.visit_ref
  1.5 13.7 %fusion.2 = bf16[64,2,128]{2,1,0:T(2,128)(2,1)} fusion(bf16[1,64,2048,128]{3,2,1,0:T(8,128)(2,1)} %param.12, f32[64,2048]{1,0:T(8,128)} %param.11, f32[2,2048]{1,0:T(2,128)} %bitcast.19), kind=kOutput, calls=%fused_computation.2 | convolution fusion | flops 67649536 | bytes 34127872 | tf_op jit(solution)/shard_map/mkcl,mklt->mkct/dot_general | solution.py:256
  15.1 17.5 %shard_map.100.coeffs_ref = bf16[4096,128]{1,0:T(8,128)(2,1)} custom-call(bf16[128,128]{1,0:T(8,128)(2,1)} %bitcast.14), custom_call_target="tpu_custom_call" | custom-call | tf_op jit(solution)/shard_map/pallas_call | solution.py:258
  32.7 37.0 %shard_map.101 = f32[64,1,256]{2,1,0:T(1,128)} custom-call(bf16[4096,128]{1,0:T(8,128)(2,1)} %shard_map.100.coeffs_ref, s32[1,128]{1,0:T(1,128)} %reshape.38.visit_ref, bf16[72,64]{1,0:T(8,128)(2,1)} %constant.4.clone.phi_table_ref, bf16[128,256]{1,0:T(8,128)(2,1)} %constant.5.clone.psi_table_ref, s32[64,1,256]{2,1,0:T(1,128)} %bitcast.16, ...), custom_call_target="tpu_custom_call" | custom-call | tf_op jit(solution)/shard_map/pallas_call | solution.py:280

commit v4 on v3

--- a/solution.py
+++ b/solution.py
@@ -32,6 +32,9 @@
         return (at_line * SQUARE + at_square) * CORES + at_core
 
     along = [(line + d) % lines for d in range(1, lines)]
+    if lines == 4:
+        half = line // 2
+        along = [line + 1 - 2 * (line % 2), 2 - half, 3 - 3 * half]
     across = [(square + d) % SQUARE for d in range(1, SQUARE)]
     other = (core + 1) % CORES
     line_peers = [index(a, square, core) for a in along]
@@ -72,7 +75,7 @@
             device_id_type=pl.DeviceIdType.MESH,
         ).wait_recv()
 
-    for peer in line_peers + square_peers + [twin]:
+    for peer in line_peers[::-1] + square_peers + [twin]:
         send(block_ref, me, peer)
     out_ref[pl.ds(pl.multiple_of(me * depth, depth), depth), :] = block_ref[...]
     for owner in line_peers:
@@ -101,7 +104,6 @@
     orders,
     order_count,
     shard_count,
-    depth,
     coeffs_ref,
     visit_ref,
     phi_table_ref,
@@ -121,13 +123,16 @@
 ):
     terms = 2 * orders
     high = PHI_T // LOW
-    theta, slots = coeffs_ref.shape[1], visit_ref.shape[1]
+    theta = coeffs_ref.shape[1]
+    depth, owners = visit_ref.shape
+    slots = owners * depth
     blocks = NPHI // (order_count * PHI_T)
     groups = slots // LANES
+    listed = jnp.concatenate([visit_ref[d : d + 1, :] for d in range(depth)], axis=1)
     for g in range(groups):
         lanes = slice(g * LANES, (g + 1) * LANES)
-        tile = jnp.maximum(visit_ref[:, lanes], 0)
-        owner = (lax.broadcasted_iota(jnp.int32, (1, LANES), 1) + g * LANES) // depth
+        tile = jnp.maximum(listed[:, lanes], 0)
+        owner = (lax.broadcasted_iota(jnp.int32, (1, LANES), 1) + g * LANES) % owners
         row = (owner % shard_count) * (theta // shard_count) + tile // blocks
         first_phi = (owner // shard_count) * (NPHI // order_count) + (tile % blocks) * PHI_T
         chosen = (
@@ -174,7 +179,8 @@
     def begin(i, values, wave):
         phi, psi = phi_ref[i], psi_ref[i]
         along_psi = fraction_ref[i][1:2]
-        key = (phi // LOW) * slots + slot_ref[i]
+        slot = slot_ref[i]
+        key = ((phi // LOW) * depth + slot % depth) * owners + slot // depth
         entry = (
             lax.broadcasted_iota(jnp.int32, (high * slots, CHUNK), 0) == key
         ).astype(jnp.float32).astype(jnp.bfloat16)
@@ -279,7 +285,7 @@
     high = PHI_T // LOW
     timeline = pl.pallas_call(
         functools.partial(
-            interpolate, modes, orders, order_count, shard_count, visits.shape[2]
+            interpolate, modes, orders, order_count, shard_count
         ),
         out_shape=jax.ShapeDtypeStruct(lined, jnp.float32),
         in_specs=[pl.BlockSpec(memory_space=pltpu.VMEM)] * 8,
@@ -295,7 +301,7 @@
         ],
     )(
         coeffs,
-        visits.reshape(1, slots),
+        jnp.transpose(visits[0]),
         phi_rows(modes),
         psi_rows(orders),
         point_slot.reshape(lined),

time: 69.9 us -> 68.6 us (0.981)
  local copies, waits for them, and re-layouts: 1.46 us -> 0 us
    unnamed x1 -> x0, local copies, waits for them, and re-layouts: 0.76 us -> none
where the time goes in v4:
time: 68.6 us; the launch traced here: 68.4 us
  Pallas kernels  54.7 us (80%)
  matrix products  13.7 us (20%)
    pallas_call x1, Pallas kernels, shards(): pl.pallas_call(functools.partial(interpolate, modes, orders, order_count,...  37.2 us
    pallas_call x1, Pallas kernels, shards(): pl.pallas_call(functools.partial(gather_blocks, shard_count // (SQUARE *...  17.5 us
    dot_general x1, matrix products, shards(): jnp.einsum('mkcl,mklt->mkct', weighted, wigner, preferred_element_type=jn...  13.7 us

profile of v4, /device:TPU:0, one launch (start us, length us, event | category | flops | bytes accessed | tf_op | source)
XLA Modules:
  0.0 68.4 jit_solution(13353121812403843078)
XLA Ops:
  0.0 13.7 %fusion.2 = bf16[64,2,128]{2,1,0:T(2,128)(2,1)} fusion(bf16[1,64,2048,128]{3,2,1,0:T(8,128)(2,1)} %param.12, f32[64,2048]{1,0:T(8,128)} %param.11, f32[2,2048]{1,0:T(2,128)} %bitcast.22), kind=kOutput, calls=%fused_computation.2 | convolution fusion | flops 67649536 | bytes 34127872 | tf_op jit(solution)/shard_map/mkcl,mklt->mkct/dot_general | solution.py:262
  13.7 17.5 %shard_map.100.coeffs_ref = bf16[4096,128]{1,0:T(8,128)(2,1)} custom-call(bf16[128,128]{1,0:T(8,128)(2,1)} %bitcast.17), custom_call_target="tpu_custom_call" | custom-call | tf_op jit(solution)/shard_map/pallas_call | solution.py:264
  31.2 37.2 %shard_map.101 = f32[64,1,256]{2,1,0:T(1,128)} custom-call(bf16[4096,128]{1,0:T(8,128)(2,1)} %shard_map.100.coeffs_ref, s32[4,32]{1,0:T(4,128)} %bitcast.23, bf16[72,64]{1,0:T(8,128)(2,1)} %constant.4.clone.phi_table_ref, bf16[128,256]{1,0:T(8,128)(2,1)} %constant.5.clone.psi_table_ref, s32[64,1,256]{2,1,0:T(1,128)} %bitcast.19, s32[64,1,256]{2,1,0:T(1,128)} %bitcast.20, ...), custom_call_target="tpu_custom_call" | custom-call | tf_op jit(solution)/shard_map/pallas_call | solution.py:286

commit v5 on v4

--- a/solution.py
+++ b/solution.py
@@ -35,10 +35,10 @@
     if lines == 4:
         half = line // 2
         along = [line + 1 - 2 * (line % 2), 2 - half, 3 - 3 * half]
-    across = [(square + d) % SQUARE for d in range(1, SQUARE)]
+    beside, above, corner = square + 1 - 2 * (square % 2), (square + 2) % SQUARE, 3 - square
     other = (core + 1) % CORES
     line_peers = [index(a, square, core) for a in along]
-    square_peers = [index(line, b, core) for b in across]
+    square_peers = [index(line, b, core) for b in (beside, above)]
     twin = index(line, square, other)
     barrier = pltpu.get_barrier_semaphore()
     peers = line_peers + square_peers + [twin]
@@ -82,13 +82,22 @@
         arrive(owner)
         for peer in square_peers + [twin]:
             send(place(owner), owner, peer)
-    for a in [line] + along:
-        for b in across:
+    for j, a in enumerate([line] + along):
+        for b, relayed, peer in (
+            (beside, j % 2 == 0, square_peers[1]),
+            (above, j % 2 == 1, square_peers[0]),
+        ):
             owner = index(a, b, core)
             arrive(owner)
+            if relayed:
+                send(place(owner), owner, peer)
             send(place(owner), owner, twin)
     for a in [line] + along:
-        for b in [square] + across:
+        owner = index(a, corner, core)
+        arrive(owner)
+        send(place(owner), owner, twin)
+    for a in [line] + along:
+        for b in (square, beside, above, corner):
             arrive(index(a, b, other))
     for copy in started:
         copy.wait_send()

time: 68.6 us -> 70 us (1.020)
  Pallas kernels: 54.7 us -> 56.2 us
    pallas_call x1, Pallas kernels: 17.5 us -> 18.9 us  [shards(): pl.pallas_call(functools.partial(gather_blocks, shard_count // (SQUARE *...]
where the time goes in v5:
time: 70 us; the launch traced here: 69.8 us
  Pallas kernels  56.2 us (80%)
  matrix products  13.7 us (20%)
    pallas_call x1, Pallas kernels, shards(): pl.pallas_call(functools.partial(interpolate, modes, orders, order_count,...  37.2 us
    pallas_call x1, Pallas kernels, shards(): pl.pallas_call(functools.partial(gather_blocks, shard_count // (SQUARE *...  18.9 us
    dot_general x1, matrix products, shards(): jnp.einsum('mkcl,mklt->mkct', weighted, wigner, preferred_element_type=jn...  13.7 us

profile of v5, /device:TPU:0, one launch (start us, length us, event | category | flops | bytes accessed | tf_op | source)
XLA Modules:
  0.0 69.8 jit_solution(1631311313622650959)
XLA Ops:
  0.0 13.7 %fusion.2 = bf16[64,2,128]{2,1,0:T(2,128)(2,1)} fusion(bf16[1,64,2048,128]{3,2,1,0:T(8,128)(2,1)} %param.12, f32[64,2048]{1,0:T(8,128)} %param.11, f32[2,2048]{1,0:T(2,128)} %bitcast.22), kind=kOutput, calls=%fused_computation.2 | convolution fusion | flops 67649536 | bytes 34127872 | tf_op jit(solution)/shard_map/mkcl,mklt->mkct/dot_general | solution.py:271
  13.7 18.9 %shard_map.100.coeffs_ref = bf16[4096,128]{1,0:T(8,128)(2,1)} custom-call(bf16[128,128]{1,0:T(8,128)(2,1)} %bitcast.17), custom_call_target="tpu_custom_call" | custom-call | tf_op jit(solution)/shard_map/pallas_call | solution.py:273
  32.6 37.2 %shard_map.101 = f32[64,1,256]{2,1,0:T(1,128)} custom-call(bf16[4096,128]{1,0:T(8,128)(2,1)} %shard_map.100.coeffs_ref, s32[4,32]{1,0:T(4,128)} %bitcast.23, bf16[72,64]{1,0:T(8,128)(2,1)} %constant.4.clone.phi_table_ref, bf16[128,256]{1,0:T(8,128)(2,1)} %constant.5.clone.psi_table_ref, s32[64,1,256]{2,1,0:T(1,128)} %bitcast.19, s32[64,1,256]{2,1,0:T(1,128)} %bitcast.20, ...), custom_call_target="tpu_custom_call" | custom-call | tf_op jit(solution)/shard_map/pallas_call | solution.py:295
